TPU v7x, 32 devices: a whole 2x2x4 slice. The times are simulated.
32 devices in a mesh: section: 4 (over x, core), dom: 8 (over z, y).
Axes of the slice: x: 2, y: 2, z: 4, core: 2. Of those that a mesh axis runs over, the one named last changes fastest.
Arguments:
- voltages: bfloat16 [512, 64, 2048], P('dom'), may hold values from -6 to 6
- station_map: int32 [512], replicated, may hold values from 0 to 511, each once
- beam_table: int32 [128, 512], replicated, may hold values from 0 to 63
- weight_table: bfloat16 [2, 64, 1024], P(None, None, 'dom'), may hold values from -0.3125 to 0.3125
- dm_trial: int32 [128], replicated, may hold values from 0 to 31
Outputs:
- power: float32 [128, 64, 1024], P(('section', 'dom'))
Inputs may be any that keep to these rules, and one draw needn't show every extreme that they name: `station_map`: each of the 512 stations appears once.
All inputs are finite; a program needn't handle non-finite values.
Results may differ from a plain program's by a relative error of at most 0.0042.
Values may be sent and summed in bfloat16 or wider, within the bound.
A program may use at most 128 MiB of HBM per device.

v0:
```python
import math

import jax
import jax.numpy as jnp
from jax import lax
from jax.sharding import PartitionSpec as P

NSTAT = 512
NFFT = 2048
CH = 1024
BEAMS = 128
NTAB = 64
FRAMES = 64
NDM = 32


def dft_table():
    sample_index = jnp.arange(NFFT, dtype=jnp.int32)
    window = 0.5 - 0.5 * jnp.cos(sample_index.astype(jnp.float32) * (2.0 * math.pi / NFFT))
    column = jnp.arange(NFFT, dtype=jnp.int32)
    bin_index = column % CH
    product = sample_index[:, None] * bin_index[None, :] % NFFT
    angle = product.astype(jnp.float32) * (2.0 * math.pi / NFFT)
    values = jnp.where(column[None, :] < CH, jnp.cos(angle), -jnp.sin(angle))
    return (values * (window[:, None] / math.sqrt(NFFT))).astype(jnp.bfloat16)


def frame_tables():
    index = jnp.arange(FRAMES, dtype=jnp.int32)
    angle = (index[:, None] * index[None, :] % FRAMES).astype(jnp.float32) * (
        2.0 * math.pi / FRAMES
    )
    cosine = jnp.cos(angle)
    sine = jnp.sin(angle)
    forward = jnp.concatenate(
        (jnp.concatenate((cosine, -sine), axis=1), jnp.concatenate((sine, cosine), axis=1)), axis=0
    )
    inverse = (
        jnp.concatenate(
            (jnp.concatenate((cosine, sine), axis=1), jnp.concatenate((-sine, cosine), axis=1)),
            axis=0,
        )
        / FRAMES
    )
    return (forward, inverse)


def dedisperse(series, trials, channels, forward, inverse):
    beam_count = series.shape[0]
    chan_count = series.shape[1]
    rows = series.reshape(beam_count * chan_count, 2 * FRAMES)
    spectrum = jnp.dot(
        rows, forward, precision=lax.Precision.HIGHEST, preferred_element_type=jnp.float32
    )
    spectrum = spectrum.reshape(beam_count, chan_count, 2, FRAMES)
    measure = (trials + 1).astype(jnp.float32) / NDM
    freq = 1.0 + channels.astype(jnp.float32) / CH
    spread = 1.0 / (freq * freq * freq)
    coeff = math.pi * measure[:, None] * spread[None, :]
    bins = jnp.arange(FRAMES, dtype=jnp.int32)
    kappa = jnp.where(bins < FRAMES // 2, bins, bins - FRAMES).astype(jnp.float32)
    phase = coeff[:, :, None] * (kappa * kappa / FRAMES)[None, None, :]
    cosine = jnp.cos(phase)
    sine = jnp.sin(phase)
    real_part = spectrum[:, :, 0] * cosine - spectrum[:, :, 1] * sine
    imag_part = spectrum[:, :, 0] * sine + spectrum[:, :, 1] * cosine
    rotated = jnp.stack((real_part, imag_part), axis=2).reshape(beam_count * chan_count, 2 * FRAMES)
    result = jnp.dot(
        rotated, inverse, precision=lax.Precision.HIGHEST, preferred_element_type=jnp.float32
    )
    result = result.reshape(beam_count, chan_count, 2, FRAMES)
    return result[:, :, 0] * result[:, :, 0] + result[:, :, 1] * result[:, :, 1]


def body(voltages, station_map, beam_table, weight_table, dm_trial):
    section_index = lax.axis_index("section")
    dom_index = lax.axis_index("dom")
    section_count = lax.axis_size("section")
    dom_count = lax.axis_size("dom")
    local_stations = voltages.shape[0]
    chan_local = weight_table.shape[2]
    per_device = BEAMS // (section_count * dom_count)
    frame_count = FRAMES // section_count
    rows_here = local_stations * frame_count
    block = lax.dynamic_slice_in_dim(voltages, section_index * frame_count, frame_count, 1)
    rows = block.reshape(rows_here, NFFT)
    spectrum = lax.dot_general(
        dft_table(), rows, (((0,), (1,)), ((), ())), preferred_element_type=jnp.float32
    )
    spectrum = spectrum.astype(jnp.bfloat16).reshape(2, CH, rows_here)
    turned = lax.all_to_all(spectrum, "dom", split_axis=1, concat_axis=2, tiled=True)
    signal = turned.reshape(2, chan_local, NSTAT, frame_count)
    arrival = jnp.take(beam_table, station_map, axis=1)
    onehot = (arrival.reshape(-1)[None, :] == jnp.arange(NTAB, dtype=jnp.int32)[:, None]).astype(
        jnp.bfloat16
    )
    mixed = jnp.einsum("rtc,tn->crn", weight_table, onehot, preferred_element_type=jnp.float32)
    weights = mixed.astype(jnp.bfloat16).reshape(chan_local, 2 * BEAMS, NSTAT)
    product = jnp.einsum("cks,rcsf->kcrf", weights, signal, preferred_element_type=jnp.float32)
    beam_re = product[:BEAMS, :, 0] - product[BEAMS:, :, 1]
    beam_im = product[:BEAMS, :, 1] + product[BEAMS:, :, 0]
    beams_now = jnp.stack((beam_re, beam_im), axis=2)
    owned = lax.all_to_all(beams_now, ("section", "dom"), split_axis=0, concat_axis=0, tiled=True)
    series = owned.reshape(section_count, dom_count, per_device, chan_local, 2, frame_count)
    series = series.transpose(2, 1, 3, 4, 0, 5).reshape(per_device, CH, 2, FRAMES)
    owner = section_index * dom_count + dom_index
    trials = lax.dynamic_slice_in_dim(dm_trial, owner * per_device, per_device, 0)
    forward, inverse = frame_tables()
    detected = dedisperse(series, trials, jnp.arange(CH, dtype=jnp.int32), forward, inverse)
    return detected.transpose(0, 2, 1)


def solution(mesh):
    in_specs = (P("dom", None, None), P(), P(), P(None, None, "dom"), P())
    out_specs = P(("section", "dom"), None, None)
    return jax.shard_map(body, mesh=mesh, in_specs=in_specs, out_specs=out_specs, check_vma=False)
```

profile of v0, /device:TPU:0, one launch (start us, length us, event | category | flops | bytes accessed | tf_op | source)
XLA Modules:
  0.0 294.5 jit_solution(16174024180362430557)
XLA Ops:
  0.1 2.5 constant_dynamic-slice_fusion
  2.6 68.6 %multiply_convert_fusion.6 = bf16[2048,2048]{1,0:T(8,128)(2,1)S(1)} fusion(f32[2048]{0:T(1024)S(1)} %subtract_multiply_fusion, s32[2048]{0:T(1024)S(1)} %add_select_fusion.2, pred[2048]{0:T(1024)(128)(4,1)S(1)} %iota_compare_fusion.1), kind=kLoop, calls=%fused_computation.9.clone.clone.clone.clone.1 | loop fusion | flops 75497472 | bytes 8407040 | tf_op jit(solution)/shard_map/dot_general | solution.py:87
  71.2 9.5 %fusion.17 = bf16[2048,1024]{1,0:T(8,128)(2,1)S(1)} fusion(bf16[1024,2048]{1,0:T(8,128)(2,1)S(1)} %bitcast.65, bf16[2048,2048]{1,0:T(8,128)(2,1)S(1)} %multiply_convert_fusion.6), kind=kOutput, calls=%fused_computation.23 | convolution fusion | flops 8592031744 | bytes 16777216 | tf_op jit(solution)/shard_map/dot_general | solution.py:87
  80.6 6.3 %copy.39 = bf16[2,1024,1024]{2,0,1:T(2,128)(2,1)} copy(bf16[2,1024,1024]{2,1,0:T(8,128)(2,1)S(1)} %bitcast.66) | data formatting | bytes 8388608 | tf_op jit(solution)/shard_map/reshape | solution.py:90
  86.9 7.4 %all-to-all-start = ((bf16[2,1024,1024]{2,0,1:T(2,128)(2,1)}), bf16[2,1024,1024]{2,0,1:T(2,128)(2,1)}, u32[]{:S(2)}, u32[]{:S(2)}) async-start(bf16[2,1024,1024]{2,0,1:T(2,128)(2,1)} %copy.39), calls=%async_computation | async-start | bytes 8388608 | tf_op jit(solution)/shard_map/all_to_all | solution.py:91
  94.5 1.0 gather_fusion
  95.9 14.7 %convolution_convert_fusion = bf16[65536,2,128]{2,0,1:T(8,128)(2,1)} fusion(bf16[2,64,128]{2,1,0:T(8,128)(2,1)S(1)} %copy-done, s32[65536]{0:T(1024)S(1)} %bitcast.67), kind=kOutput, calls=%fused_computation.1 | convolution fusion | flops 2168455168 | bytes 33849344 | tf_op jit(solution)/shard_map/rtc,tn->crn/dot_general | solution.py:97
  110.7 44.3 %copy.50 = bf16[128,256,512,1]{2,1,3,0:T(8,128)(2,1)} copy(bf16[128,256,512,1]{0,2,1,3:T(8,128)(2,1)} %bitcast.60) | data formatting | bytes 67108864 | tf_op jit(solution)/shard_map/reshape | solution.py:98
  154.9 32.7 %all-to-all-done = bf16[2,1024,1024]{2,0,1:T(2,128)(2,1)} async-done(((bf16[2,1024,1024]{2,0,1:T(2,128)(2,1)}), bf16[2,1024,1024]{2,0,1:T(2,128)(2,1)}, u32[]{:S(2)}, u32[]{:S(2)}) %all-to-all-start) | async-done | bytes 4194336 | tf_op jit(solution)/shard_map/all_to_all | solution.py:91
  187.6 5.6 %copy.40 = bf16[2,1024,1024]{2,1,0:T(8,128)(2,1)} copy(bf16[2,1024,1024]{2,0,1:T(2,128)(2,1)} %all-to-all-done) | data formatting | bytes 8388608 | tf_op jit(solution)/shard_map/all_to_all | solution.py:91
  193.2 6.2 %copy.41 = bf16[2,128,8,1024]{1,3,2,0:T(8,128)(2,1)} copy(bf16[2,128,8,1024]{3,1,2,0:T(8,128)(2,1)} %bitcast.61) | data formatting | bytes 8388608 | tf_op jit(solution)/shard_map/all_to_all | solution.py:91
  199.4 8.6 %copy.44 = bf16[2,128,512,16]{2,3,0,1:T(8,128)(2,1)} copy(bf16[2,128,512,16]{1,3,2,0:T(8,128)(2,1)} %bitcast.62) | data formatting | bytes 8388608 | tf_op jit(solution)/shard_map/reshape | solution.py:92
  208.0 16.0 %convolution_bitcast_fusion = f32[256,128,2,16]{0,3,2,1:T(8,128)S(1)} fusion(bf16[2,128,512,16]{2,3,0,1:T(8,128)(2,1)} %copy.44, bf16[128,256,512,1]{2,1,3,0:T(8,128)(2,1)} %copy.50), kind=kOutput, calls=%fused_computation.24 | convolution fusion | flops 1073741824 | bytes 41943040 | tf_op jit(solution)/shard_map/cks,rcsf->kcrf/dot_general | solution.py:99
  224.0 0.3 slice_subtract_fusion
  224.5 2.3 copy.46
  226.8 3.9 %all-to-all-start.1 = ((f32[128,128,2,16]{1,3,2,0:T(8,128)}), f32[128,128,2,16]{1,3,2,0:T(8,128)S(1)}, u32[]{:S(2)}, u32[]{:S(2)}) async-start(f32[128,128,2,16]{1,3,2,0:T(8,128)} %copy.46), calls=%async_computation.1 | async-start | bytes 4194304 | tf_op jit(solution)/shard_map/all_to_all | solution.py:103
  231.3 49.2 %all-to-all-done.1 = f32[128,128,2,16]{1,3,2,0:T(8,128)S(1)} async-done(((f32[128,128,2,16]{1,3,2,0:T(8,128)}), f32[128,128,2,16]{1,3,2,0:T(8,128)S(1)}, u32[]{:S(2)}, u32[]{:S(2)}) %all-to-all-start.1) | async-done | bytes 2097184 | tf_op jit(solution)/shard_map/all_to_all | solution.py:103
  280.5 2.5 copy.47
  283.1 1.7 dot_general.30
  284.8 2.1 fusion.18
  286.9 4.0 %fusion.24 = (f32[4,1024,1,64]{1,3,2,0:T(8,128)S(1)}, f32[4,1024,1,64]{1,3,2,0:T(8,128)S(1)}) fusion(f32[4,1024,2,64]{1,3,2,0:T(8,128)S(1)} %fusion.18, f32[64]{0:T(128)S(1)} %fusion.46, f32[4,1024]{1,0:T(4,128)S(1)} %broadcast_multiply_fusion), kind=kLoop, calls=%fused_computation.35 | loop fusion | flops 1835008 | bytes 4210944 | tf_op jit(solution)/shard_map/sub | solution.py:65
  291.0 0.2 pad_maximum_fusion.1
  291.2 2.1 fusion.51
  293.4 1.1 fusion.27
  (28 shorter events, 1.3 us)
Async XLA Ops:
  0.0 95.9 %copy-start = (bf16[2,64,128]{2,1,0:T(8,128)(2,1)S(1)}, bf16[2,64,128]{2,1,0:T(8,128)(2,1)}, u32[]{:S(2)}) copy-start(bf16[2,64,128]{2,1,0:T(8,128)(2,1)} %param.8) | copy-start | bytes 98308
  86.9 7.4 %copy-start.2 = (s32[128,512]{1,0:T(8,128)S(1)}, s32[128,512]{1,0:T(8,128)}, u32[]{:S(2)}) copy-start(s32[128,512]{1,0:T(8,128)} %param.7) | copy-start | bytes 786436
  86.9 7.6 %copy-start.3 = (s32[512]{0:T(512)S(1)}, s32[512]{0:T(512)}, u32[]{:S(2)}) copy-start(s32[512]{0:T(512)} %param.6) | copy-start | bytes 6148
  86.9 100.7 %all-to-all-start = ((bf16[2,1024,1024]{2,0,1:T(2,128)(2,1)}), bf16[2,1024,1024]{2,0,1:T(2,128)(2,1)}, u32[]{:S(2)}, u32[]{:S(2)}) async-start(bf16[2,1024,1024]{2,0,1:T(2,128)(2,1)} %copy.39), calls=%async_computation | async-start | bytes 8388608 | tf_op jit(solution)/shard_map/all_to_all | solution.py:91
  224.5 6.3 %copy-start.4 = (s32[128]{0:T(128)S(1)}, s32[128]{0:T(128)}, u32[]{:S(2)}) copy-start(s32[128]{0:T(128)} %param.9) | copy-start | bytes 1540
  226.8 53.7 %all-to-all-start.1 = ((f32[128,128,2,16]{1,3,2,0:T(8,128)}), f32[128,128,2,16]{1,3,2,0:T(8,128)S(1)}, u32[]{:S(2)}, u32[]{:S(2)}) async-start(f32[128,128,2,16]{1,3,2,0:T(8,128)} %copy.46), calls=%async_computation.1 | async-start | bytes 4194304 | tf_op jit(solution)/shard_map/all_to_all | solution.py:103
  291.0 3.6 %copy-start.1 = (bf16[2,64,128]{2,1,0:T(8,128)(2,1)S(1)}, bf16[2,64,128]{2,1,0:T(8,128)(2,1)}, u32[]{:S(2)}) copy-start(bf16[2,64,128]{2,1,0:T(8,128)(2,1)} %param.8) | copy-start | bytes 98308
where the time goes:
time: 296 us; the launch traced here: 295 us
  waiting for transfers between devices  81.9 us (28%)
  local copies, waits for them, and re-layouts  81.4 us (28%)
  other arithmetic  75.2 us (25%)
  matrix products  44.5 us (15%)
  starting transfers between devices  11.3 us (4%)
    dot_general x1, other arithmetic, body(): lax.dot_general(dft_table(), rows, (((0,), (1,)), ((), ())), preferred_el...  68.6 us
    all_to_all x1, waiting for transfers between devices, body(): lax.all_to_all(beams_now, ('section', 'dom'), split_axis=0, concat_axis=0...  49.2 us
    reshape x1, local copies, waits for them, and re-layouts, body(): weights = mixed.astype(jnp.bfloat16).reshape(chan_local, 2 * BEAMS, NSTAT)  44.3 us
    all_to_all x1, waiting for transfers between devices, body(): lax.all_to_all(spectrum, 'dom', split_axis=1, concat_axis=2, tiled=True)  32.7 us
    dot_general x1, matrix products, body(): jnp.einsum('cks,rcsf->kcrf', weights, signal, preferred_element_type=jnp....  16 us
    dot_general x1, matrix products, body(): jnp.einsum('rtc,tn->crn', weight_table, onehot, preferred_element_type=jn...  14.7 us
    all_to_all x2, local copies, waits for them, and re-layouts, body(): lax.all_to_all(spectrum, 'dom', split_axis=1, concat_axis=2, tiled=True)  11.8 us
    dot_general x1, matrix products, body(): lax.dot_general(dft_table(), rows, (((0,), (1,)), ((), ())), preferred_el...  9.45 us
  transfers between devices with their start and end apart: 2, of which 2 were waited for; matrix products, arithmetic and copies ran while one was open for 21% of the time, Pallas kernels for 0%

commit v1 on v0

v1 whole, which is shorter than its diff:
```python
import math

import jax
import jax.numpy as jnp
from jax import lax
from jax.experimental import pallas as pl
from jax.experimental.pallas import tpu as pltpu
from jax.sharding import PartitionSpec as P

NFFT = 2048
CH = 1024
NTAB = 64
NDM = 32
LANES = 128
TILE = 64


def phasor_rows(steps, channels):
    product = steps[:, None] * channels[None, :] % NFFT
    angle = product.astype(jnp.float32) * (2.0 * math.pi / NFFT)
    return jnp.cos(angle), jnp.sin(angle)


def dft_columns(channels, is_imag):
    fine = 64
    coarse = NFFT // fine
    cos_a, sin_a = phasor_rows(fine * jnp.arange(coarse, dtype=jnp.int32), channels)
    cos_b, sin_b = phasor_rows(jnp.arange(fine, dtype=jnp.int32), channels)
    first = jnp.where(is_imag[None, :], -sin_a, cos_a)
    second = jnp.where(is_imag[None, :], -cos_a, -sin_a)
    sample = jnp.arange(NFFT, dtype=jnp.int32).astype(jnp.float32)
    window = 0.5 - 0.5 * jnp.cos(sample * (2.0 * math.pi / NFFT))
    window = window.reshape(coarse, fine) / math.sqrt(NFFT)
    first, second, cos_b, sin_b, window = lax.optimization_barrier(
        (first, second, cos_b, sin_b, window)
    )
    values = first[:, None, :] * cos_b[None] + second[:, None, :] * sin_b[None]
    values = values * window[:, :, None]
    return values.astype(jnp.bfloat16).reshape(NFFT, channels.shape[0])


def split_bf16(values):
    high = lax.reduce_precision(values, 8, 7)
    return high.astype(jnp.bfloat16), (values - high).astype(jnp.bfloat16)


def frame_matrices(frames, sections, groups):
    index = jnp.arange(frames, dtype=jnp.int32)
    angle = (index[:, None] * index[None, :] % frames).astype(jnp.float32) * (
        2.0 * math.pi / frames
    )
    cosine = jnp.cos(angle)
    sine = jnp.sin(angle)
    local = frames // sections
    forward = jnp.stack((jnp.stack((cosine, sine), 1), jnp.stack((-sine, cosine), 1)), 0)
    forward = forward.reshape(2 * frames, 2, sections, local).transpose(0, 2, 1, 3)
    forward = jnp.broadcast_to(
        forward[:, :, None], (2 * frames, sections, groups, 2, local)
    ).reshape(2 * frames, groups * 2 * frames)
    inverse = jnp.stack((jnp.stack((cosine, -sine), 1), jnp.stack((sine, cosine), 1)), 0)
    inverse = inverse.reshape(2 * frames, 2 * frames) / frames
    return split_bf16(forward) + split_bf16(inverse)


def pick_lanes(entries, where):
    dims = lax.GatherDimensionNumbers(
        offset_dims=(),
        collapsed_slice_dims=(1,),
        start_index_map=(1,),
        operand_batching_dims=(0,),
        start_indices_batching_dims=(0,),
    )
    return lax.gather(
        entries,
        where[..., None],
        dims,
        slice_sizes=(1, 1),
        mode=lax.GatherScatterMode.PROMISE_IN_BOUNDS,
    )


def weight_kernel(table_ref, index_ref, out_ref):
    stations, beams = index_ref.shape
    count = table_ref.shape[0]
    for tile in range(stations // TILE):
        span = pl.ds(tile * TILE, TILE)
        real_at = index_ref[span, :]
        imag_at = real_at + NTAB
        for chan in range(count):
            entry = jnp.broadcast_to(table_ref[pl.ds(chan, 1), :], (TILE, LANES))
            for part, where in enumerate((real_at, imag_at)):
                picked = pick_lanes(entry, where)
                out_ref[chan, span, pl.ds(part * beams, beams)] = picked.astype(jnp.bfloat16)


def station_weights(table, index):
    stations, beams = index.shape
    chans = table.shape[0]
    block = min(8, chans)
    return pl.pallas_call(
        weight_kernel,
        grid=(chans // block,),
        in_specs=[
            pl.BlockSpec((block, LANES), lambda i: (i, 0)),
            pl.BlockSpec((stations, beams), lambda i: (0, 0)),
        ],
        out_specs=pl.BlockSpec((block, stations, 2 * beams), lambda i: (i, 0, 0)),
        out_shape=jax.ShapeDtypeStruct((chans, stations, 2 * beams), jnp.bfloat16),
        cost_estimate=pl.CostEstimate(
            flops=0, bytes_accessed=chans * 2 * beams * stations * 5, transcendentals=0
        ),
        name="station_weights",
    )(table, index)


def beam_kernel(signal_ref, weight_ref, out_ref):
    count, depth, _ = signal_ref.shape
    beams = out_ref.shape[2]
    half = depth // 2
    for chan in range(count):
        product = jnp.dot(
            signal_ref[chan], weight_ref[chan], preferred_element_type=jnp.float32
        )
        real = product[:half, :beams] - product[half:, beams:]
        imag = product[half:, :beams] + product[:half, beams:]
        out_ref[chan, :half] = real.astype(jnp.bfloat16)
        out_ref[chan, half:] = imag.astype(jnp.bfloat16)


def form_beams(signal, weights):
    chans, depth, held = signal.shape
    beams = weights.shape[2] // 2
    block = min(16, chans)
    return pl.pallas_call(
        beam_kernel,
        grid=(chans // block,),
        in_specs=[
            pl.BlockSpec((block, depth, held), lambda i: (i, 0, 0)),
            pl.BlockSpec((block, held, 2 * beams), lambda i: (i, 0, 0)),
        ],
        out_specs=pl.BlockSpec((block, depth, beams), lambda i: (i, 0, 0)),
        out_shape=jax.ShapeDtypeStruct((chans, depth, beams), jnp.bfloat16),
        cost_estimate=pl.CostEstimate(
            flops=chans * depth * held * beams * 4,
            bytes_accessed=chans * held * beams * 6,
            transcendentals=0,
        ),
        name="form_beams",
    )(signal, weights)


def dedisperse_kernel(x_ref, cos_ref, sin_ref, fh_ref, fl_ref, ih_ref, il_ref, *rest):
    out_ref = rest[-1]
    sections, groups, blocks, _, depth, chans = x_ref.shape
    frames = cos_ref.shape[1]

    def dot(a, b):
        return jnp.dot(a, b, preferred_element_type=jnp.float32)

    for block in range(blocks):
        span = pl.ds(block * chans, chans)
        x = x_ref[:, :, block, 0].reshape(sections * groups * depth, chans)
        spec = dot(fh_ref[...], x) + dot(fl_ref[...], x)
        cosine = cos_ref[0, :, span]
        sine = sin_ref[0, :, span]
        real = spec[:frames] * cosine - spec[frames:] * sine
        imag = spec[:frames] * sine + spec[frames:] * cosine
        turned = jnp.concatenate((real, imag), axis=0)
        high = turned.astype(jnp.bfloat16)
        low = (turned - high.astype(jnp.float32)).astype(jnp.bfloat16)
        y = dot(ih_ref[...], high) + dot(ih_ref[...], low) + dot(il_ref[...], high)
        out_ref[0, :, span] = y[:frames] * y[:frames] + y[frames:] * y[frames:]


def dedisperse(series, cosine, sine, matrices, chunk, chunks, partial):
    sections, groups, blocks, beams, depth, chans = series.shape
    frames = cosine.shape[1]
    wide = blocks * chans
    whole = [pl.BlockSpec(m.shape, lambda i: (0, 0)) for m in matrices]
    tables = pl.BlockSpec((1, frames, wide), lambda i: (i, 0, 0))
    earlier = [] if partial is None else [partial]
    return pl.pallas_call(
        dedisperse_kernel,
        grid=(beams,),
        in_specs=[
            pl.BlockSpec(
                (sections, groups, blocks, 1, depth, chans), lambda i: (0, 0, 0, i, 0, 0)
            ),
            tables,
            tables,
        ]
        + whole
        + [pl.BlockSpec(memory_space=pl.ANY) for _ in earlier],
        out_specs=pl.BlockSpec((1, frames, wide), lambda i: (i, 0, chunk)),
        out_shape=jax.ShapeDtypeStruct((beams, frames, wide * chunks), jnp.float32),
        input_output_aliases={7: 0} if earlier else {},
        cost_estimate=pl.CostEstimate(
            flops=beams * wide * 2 * frames * 2 * frames * 14,
            bytes_accessed=beams * wide * frames * 16,
            transcendentals=0,
        ),
        name="dedisperse",
    )(series, cosine, sine, *matrices, *earlier)


def body(voltages, station_map, beam_table, weight_table, dm_trial):
    section_index = lax.axis_index("section")
    dom_index = lax.axis_index("dom")
    sections = lax.axis_size("section")
    doms = lax.axis_size("dom")
    groups = 2
    peers = doms // groups
    group_index = dom_index // peers
    stations = voltages.shape[0]
    frames = voltages.shape[1]
    beams = beam_table.shape[0]
    chans = weight_table.shape[2]
    per_device = beams // (sections * doms)
    local = frames // sections
    rows_here = stations * local
    station_groups = [[g * peers + p for p in range(peers)] for g in range(groups)]

    swapped = lax.ppermute(weight_table, "dom", [(d, (d + peers) % doms) for d in range(doms)])
    block = lax.dynamic_slice_in_dim(voltages, section_index * local, local, 1)
    rows = block.reshape(rows_here, NFFT)

    held = stations * peers
    mine = lax.dynamic_slice_in_dim(station_map, group_index * held, held, 0)
    arrival = jnp.take(beam_table, mine, axis=1, mode="clip").T
    swapped, rows = lax.optimization_barrier((swapped, rows))

    column = jnp.arange(peers * 2 * chans, dtype=jnp.int32)
    column_chan = column // (2 * chans) * chans + column % chans
    is_imag = column // chans % 2 == 1

    owner = section_index * doms + dom_index
    trials = lax.dynamic_slice_in_dim(dm_trial, owner * per_device, per_device, 0)
    measure = (trials + 1).astype(jnp.float32) / NDM
    bins = jnp.arange(frames, dtype=jnp.int32)
    kappa = jnp.where(bins < frames // 2, bins, bins - frames).astype(jnp.float32)
    matrices = frame_matrices(frames, sections, groups)

    sent = []
    for chunk in range(groups):
        table = dft_columns(chunk * peers * chans + column_chan, is_imag)
        spectrum = lax.dot_general(
            table, rows, (((0,), (1,)), ((), ())), preferred_element_type=jnp.float32
        )
        spectrum = spectrum.astype(jnp.bfloat16).reshape(peers, 2 * chans, rows_here)
        sent.append(
            lax.all_to_all(
                spectrum,
                "dom",
                split_axis=0,
                concat_axis=0,
                axis_index_groups=station_groups,
                tiled=True,
            )
        )
    power = None
    for chunk in range(groups):
        owned_table = jnp.where(group_index == chunk, weight_table, swapped)
        lookup = owned_table.transpose(2, 0, 1).reshape(chans, 2 * NTAB).astype(jnp.float32)
        weights = station_weights(lookup, arrival)
        signal = sent[chunk].reshape(peers, 2, chans, stations, local)
        signal = signal.transpose(2, 1, 4, 0, 3).reshape(chans, 2 * local, held)
        series = form_beams(signal, weights).transpose(2, 1, 0)
        series = series.reshape(sections * doms, per_device, 2 * local, chans)
        owned = lax.all_to_all(
            series, ("section", "dom"), split_axis=0, concat_axis=0, tiled=True
        )
        owned = owned.reshape(sections, groups, peers, per_device, 2 * local, chans)
        channels = chunk * peers * chans + jnp.arange(peers * chans, dtype=jnp.int32)
        freq = 1.0 + channels.astype(jnp.float32) / CH
        spread = 1.0 / (freq * freq * freq)
        coeff = math.pi * measure[:, None] * spread[None, :]
        phase = coeff[:, None, :] * (kappa * kappa / frames)[None, :, None]
        power = dedisperse(
            owned, jnp.cos(phase), jnp.sin(phase), matrices, chunk, groups, power
        )
    return power


def solution(mesh):
    in_specs = (P("dom", None, None), P(), P(), P(None, None, "dom"), P())
    out_specs = P(("section", "dom"), None, None)
    return jax.shard_map(body, mesh=mesh, in_specs=in_specs, out_specs=out_specs, check_vma=False)
```

time: 296 us -> 176 us (0.59)
  Pallas kernels: 0 us -> 64.5 us
  other arithmetic: 75.2 us -> 13.7 us
  waiting for transfers between devices: 81.9 us -> 24.8 us
  local copies, waits for them, and re-layouts: 81.4 us -> 38.6 us
  matrix products: 44.5 us -> 10.7 us
  starting transfers between devices: 11.3 us -> 22.3 us
    dot_general x1 -> x0, other arithmetic: 68.6 us -> none  [body(): lax.dot_general(dft_table(), rows, (((0,), (1,)), ((), ())), preferred_el...]
    pallas_call x0 -> x6, Pallas kernels: none -> 64.5 us  [the longest x2 32.1 us: station_weights(): pl.pallas_call(weight_kernel, grid=(chans // block,), in_specs=[pl.BlockS...]
    all_to_all x2 -> x4, waiting for transfers between devices: 81.9 us -> 24.8 us  [the longest x2 14.5 us: body(): lax.all_to_all(series, ('section', 'dom'), split_axis=0, concat_axis=0, t...]
    reshape x3 -> x8, local copies, waits for them, and re-layouts: 59.1 us -> 19.1 us  [the longest x2 7.62 us: body(): signal = signal.transpose(2, 1, 4, 0, 3).reshape(chans, 2 * local, held)]
    dot_general x5 -> x2, matrix products: 44.5 us -> 10.7 us  [body(): lax.dot_general(table, rows, (((0,), (1,)), ((), ())), preferred_element_...]
    all_to_all x2 -> x0, local copies, waits for them, and re-layouts: 11.8 us -> none  [body(): lax.all_to_all(spectrum, 'dom', split_axis=1, concat_axis=2, tiled=True)]
    transpose x1 -> x5, local copies, waits for them, and re-layouts: 2.55 us -> 10.9 us  [the longest x2 6.42 us: body(): series = form_beams(signal, weights).transpose(2, 1, 0)]
    all_to_all x2 -> x4, starting transfers between devices: 11.3 us -> 18.2 us  [the longest x2 9.98 us: body(): lax.all_to_all(series, ('section', 'dom'), split_axis=0, concat_axis=0, t...]
  transfers between devices with their start and end apart: 2 -> 5, of which waited for: 2 -> 2; matrix products, arithmetic and copies ran while one was open for 21% -> 30% of each run, Pallas kernels for 0% -> 34%
where the time goes in v1:
time: 176 us; the launch traced here: 175 us
  Pallas kernels  64.5 us (37%)
  local copies, waits for them, and re-layouts  38.6 us (22%)
  waiting for transfers between devices  24.8 us (14%)
  starting transfers between devices  22.3 us (13%)
  other arithmetic  13.7 us (8%)
  matrix products  10.7 us (6%)
    pallas_call x2, Pallas kernels, station_weights(): pl.pallas_call(weight_kernel, grid=(chans // block,), in_specs=[pl.BlockS...  32.1 us
    pallas_call x2, Pallas kernels, form_beams(): pl.pallas_call(beam_kernel, grid=(chans // block,), in_specs=[pl.BlockSpe...  21.2 us
    all_to_all x2, waiting for transfers between devices, body(): lax.all_to_all(series, ('section', 'dom'), split_axis=0, concat_axis=0, t...  14.5 us
    pallas_call x2, Pallas kernels, dedisperse(): pl.pallas_call(dedisperse_kernel, grid=(beams,), in_specs=[pl.BlockSpec((...  11.1 us
    dot_general x2, matrix products, body(): lax.dot_general(table, rows, (((0,), (1,)), ((), ())), preferred_element_...  10.7 us
    all_to_all x2, waiting for transfers between devices, body(): lax.all_to_all(spectrum, 'dom', split_axis=0, concat_axis=0, axis_index_g...  10.3 us
    all_to_all x2, starting transfers between devices, body(): lax.all_to_all(series, ('section', 'dom'), split_axis=0, concat_axis=0, t...  9.98 us
    all_to_all x2, starting transfers between devices, body(): lax.all_to_all(spectrum, 'dom', split_axis=0, concat_axis=0, axis_index_g...  8.26 us
  transfers between devices with their start and end apart: 5, of which 2 were waited for; matrix products, arithmetic and copies ran while one was open for 30% of the time, Pallas kernels for 34%

profile of v1, /device:TPU:0, one launch (start us, length us, event | category | flops | bytes accessed | tf_op | source)
XLA Modules:
  0.0 174.8 jit_solution(11084180051579373142)
XLA Ops:
  0.0 4.1 %collective-permute-start = (bf16[2,64,128]{2,1,0:T(8,128)(2,1)}, bf16[2,64,128]{2,1,0:T(8,128)(2,1)S(1)}, u32[]{:S(2)}, u32[]{:S(2)}) collective-permute-start(bf16[2,64,128]{2,1,0:T(8,128)(2,1)} %param.8), channel_id=1, source_target_pairs={{0,4},{1,5},{2,6},{3,7},{4,0},{5,1},{6,2},{7,3},{8,12},{9,13},{10,... | collective-permute-start | bytes 98312 | tf_op jit(solution)/shard_map/ppermute | solution.py:223
  8.2 2.5 %constant_dynamic-slice_fusion = bf16[64,16,2048]{2,1,0:T(8,128)(2,1)S(1)} fusion(bf16[64,64,2048]{2,1,0:T(8,128)(2,1)} %param.5, s32[]{:T(128)S(6)} %select_n.202), kind=kLoop, calls=%fused_computation.125 | loop fusion | bytes 8388612 | tf_op jit(solution)/shard_map/dynamic_slice | solution.py:224
  10.7 4.8 %convolution_convert_fusion = bf16[1024,1024]{1,0:T(8,128)(2,1)S(1)} fusion(bf16[2048,1024]{1,0:T(8,128)(2,1)S(1)} %fusion, bf16[1024,2048]{1,0:T(8,128)(2,1)S(1)} %bitcast.54), kind=kOutput, calls=%fused_computation.7 | convolution fusion | flops 4296015872 | bytes 10485760 | tf_op jit(solution)/shard_map/dot_general | solution.py:246
  15.6 2.6 %copy.24 = bf16[4,256,1024]{1,2,0:T(8,128)(2,1)} copy(bf16[4,256,1024]{2,1,0:T(8,128)(2,1)S(1)} %bitcast.58) | data formatting | bytes 4194304 | tf_op jit(solution)/shard_map/reshape | solution.py:249
  18.2 3.8 %all-to-all-start.2 = ((bf16[4,256,1024]{1,2,0:T(8,128)(2,1)}), bf16[4,256,1024]{1,2,0:T(8,128)(2,1)S(1)}, u32[]{:S(2)}, u32[]{:S(2)}) async-start(bf16[4,256,1024]{1,2,0:T(8,128)(2,1)} %copy.24), calls=%async_computation.2 | async-start | bytes 4194304 | tf_op jit(solution)/shard_map/all_to_all | solution.py:251
  26.5 5.8 %convolution_convert_fusion.1 = bf16[1024,1024]{1,0:T(8,128)(2,1)} fusion(bf16[2048,1024]{1,0:T(8,128)(2,1)S(1)} %fusion.1, bf16[1024,2048]{1,0:T(8,128)(2,1)S(1)} %bitcast.55), kind=kOutput, calls=%fused_computation.8 | convolution fusion | flops 4296015872 | bytes 10485760 | tf_op jit(solution)/shard_map/dot_general | solution.py:246
  32.4 4.0 %copy.13 = bf16[4,256,1024]{1,2,0:T(8,128)(2,1)} copy(bf16[4,256,1024]{2,1,0:T(8,128)(2,1)} %bitcast.57) | data formatting | bytes 4194304 | tf_op jit(solution)/shard_map/reshape | solution.py:249
  36.3 10.3 %all-to-all-done.2 = bf16[4,256,1024]{1,2,0:T(8,128)(2,1)S(1)} async-done(((bf16[4,256,1024]{1,2,0:T(8,128)(2,1)}), bf16[4,256,1024]{1,2,0:T(8,128)(2,1)S(1)}, u32[]{:S(2)}, u32[]{:S(2)}) %all-to-all-start.2) | async-done | bytes 2097184 | tf_op jit(solution)/shard_map/all_to_all | solution.py:251
  46.6 4.5 %all-to-all-start = ((bf16[4,256,1024]{1,2,0:T(8,128)(2,1)}), bf16[4,256,1024]{1,2,0:T(8,128)(2,1)}, u32[]{:S(2)}, u32[]{:S(2)}) async-start(bf16[4,256,1024]{1,2,0:T(8,128)(2,1)} %copy.13), calls=%async_computation | async-start | bytes 4194304 | tf_op jit(solution)/shard_map/all_to_all | solution.py:251
  53.5 16.1 %station_weights.3.weight_ref = bf16[128,256,256]{2,1,0:T(8,128)(2,1)} custom-call(f32[128,128]{1,0:T(8,128)} %copy.26.table_ref, s32[256,128]{1,0:T(8,128)} %gather_fusion), custom_call_target="tpu_custom_call" | custom-call | bytes 41943040 | tf_op jit(solution)/shard_map/station_weights/pallas_call | solution.py:100
  74.0 3.0 %copy.27.signal_ref = bf16[128,32,256]{2,1,0:T(8,128)(2,1)} copy(bf16[128,32,256]{0,2,1:T(8,128)(2,1)S(1)} %bitcast.48) | data formatting | bytes 4194304 | tf_op jit(solution)/shard_map/reshape | solution.py:266
  77.0 10.6 %form_beams.3 = bf16[128,32,128]{2,1,0:T(8,128)(2,1)} custom-call(bf16[128,32,256]{2,1,0:T(8,128)(2,1)} %copy.27.signal_ref, bf16[128,256,256]{2,1,0:T(8,128)(2,1)} %station_weights.3.weight_ref), custom_call_target="tpu_custom_call" | custom-call | flops 536870912 | bytes 25165824 | tf_op jit(solution)/shard_map/form_beams/pallas_call | solution.py:134
  87.6 3.2 %copy.28 = bf16[128,32,128]{2,1,0:T(8,128)(2,1)} copy(bf16[128,32,128]{0,1,2:T(8,128)(2,1)} %bitcast.52) | data formatting | bytes 2097152 | tf_op jit(solution)/shard_map/transpose | solution.py:267
  90.8 4.4 %all-to-all-start.3 = ((bf16[32,4,32,128]{3,2,1,0:T(8,128)(2,1)}), bf16[32,4,32,128]{3,2,1,0:T(8,128)(2,1)S(1)}, u32[]{:S(2)}, u32[]{:S(2)}) async-start(bf16[32,4,32,128]{3,2,1,0:T(8,128)(2,1)} %bitcast.24), calls=%async_computation.3 | async-start | bytes 2097152 | tf_op jit(solution)/shard_map/all_to_all | solution.py:269
  95.9 16.1 %station_weights.2.weight_ref = bf16[128,256,256]{2,1,0:T(8,128)(2,1)} custom-call(f32[128,128]{1,0:T(8,128)} %copy.16.table_ref, s32[256,128]{1,0:T(8,128)} %gather_fusion), custom_call_target="tpu_custom_call" | custom-call | bytes 41943040 | tf_op jit(solution)/shard_map/station_weights/pallas_call | solution.py:100
  112.0 2.5 %reshape.287 = bf16[4,2,128,64,16]{2,1,4,3,0:T(2,128)(2,1)S(1)} reshape(bf16[4,256,1024]{1,2,0:T(8,128)(2,1)} %all-to-all-done) | data formatting | bytes 4194304 | tf_op jit(solution)/shard_map/reshape | solution.py:265
  116.7 4.6 %copy.17.signal_ref = bf16[128,32,256]{2,1,0:T(8,128)(2,1)} copy(bf16[128,32,256]{0,2,1:T(8,128)(2,1)} %bitcast.50) | data formatting | bytes 4194304 | tf_op jit(solution)/shard_map/reshape | solution.py:266
  121.3 10.6 %form_beams.2 = bf16[128,32,128]{2,1,0:T(8,128)(2,1)} custom-call(bf16[128,32,256]{2,1,0:T(8,128)(2,1)} %copy.17.signal_ref, bf16[128,256,256]{2,1,0:T(8,128)(2,1)} %station_weights.2.weight_ref), custom_call_target="tpu_custom_call" | custom-call | flops 536870912 | bytes 25165824 | tf_op jit(solution)/shard_map/form_beams/pallas_call | solution.py:134
  131.9 3.2 %copy.18 = bf16[128,32,128]{2,1,0:T(8,128)(2,1)} copy(bf16[128,32,128]{0,1,2:T(8,128)(2,1)} %bitcast.53) | data formatting | bytes 2097152 | tf_op jit(solution)/shard_map/transpose | solution.py:267
  135.1 5.6 %all-to-all-start.1 = ((bf16[32,4,32,128]{3,2,1,0:T(8,128)(2,1)}), bf16[32,4,32,128]{3,2,1,0:T(8,128)(2,1)S(1)}, u32[]{:S(2)}, u32[]{:S(2)}) async-start(bf16[32,4,32,128]{3,2,1,0:T(8,128)(2,1)} %bitcast.8), calls=%async_computation.1 | async-start | bytes 2097152 | tf_op jit(solution)/shard_map/all_to_all | solution.py:269
  143.3 4.9 %multiply_sine_fusion = (f32[4,64,512]{2,1,0:T(8,128)}, f32[4,64,512]{2,1,0:T(8,128)}, f32[4,64,512]{2,1,0:T(8,128)}, f32[4,64,512]{2,1,0:T(8,128)}) fusion(f32[4,512]{1,0:T(4,128)S(1)} %get-tuple-element.57, f32[64]{0:T(128)S(1)} %fusion.58, f32[4,512]{1,0:T(4,128)S(1)} %get-tuple-element.58), kind=kLoop, calls=%fused_computation.9 | loop fusion | flops 262144 | bytes 2113792 | tf_op jit(solution)/shard_map/sin | solution.py:279
  148.1 5.6 %dedisperse.2.rest_0_ = f32[4,64,1024]{2,1,0:T(8,128)} custom-call(bf16[4,2,4,4,32,128]{5,4,3,2,1,0:T(8,128)(2,1)} %bitcast.51, f32[4,64,512]{2,1,0:T(8,128)} %get-tuple-element.42.cos_ref, f32[4,64,512]{2,1,0:T(8,128)} %get-tuple-element.41.sin_ref, bf16[128,256]{1,0:T(8,128)(2,1)} %get-tuple-element.30.fh_ref, bf16[128,256]{1,0:T(8,128)(2,1)} %get-tuple-element.29.fl_ref, ...), custom_call_target="tpu_custom_call" | custom-call | flops 469762048 | bytes 2097152 | tf_op jit(solution)/shard_map/dedisperse/pallas_call | solution.py:182
  153.7 14.5 %all-to-all-done.1 = bf16[32,4,32,128]{3,2,1,0:T(8,128)(2,1)S(1)} async-done(((bf16[32,4,32,128]{3,2,1,0:T(8,128)(2,1)}), bf16[32,4,32,128]{3,2,1,0:T(8,128)(2,1)S(1)}, u32[]{:S(2)}, u32[]{:S(2)}) %all-to-all-start.1) | async-done | bytes 1048608 | tf_op jit(solution)/shard_map/all_to_all | solution.py:269
  169.2 5.6 %dedisperse.3 = f32[4,64,1024]{2,1,0:T(8,128)} custom-call(bf16[4,2,4,4,32,128]{5,4,3,2,1,0:T(8,128)(2,1)} %bitcast.56, f32[4,64,512]{2,1,0:T(8,128)} %get-tuple-element.55.cos_ref, f32[4,64,512]{2,1,0:T(8,128)} %get-tuple-element.56.sin_ref, bf16[128,256]{1,0:T(8,128)(2,1)} %get-tuple-element.30.fh_ref, ...), custom_call_target="tpu_custom_call", output_to_operand_aliasing={{}: (7, {})} | custom-call | flops 469762048 | bytes 2097152 | tf_op jit(solution)/shard_map/dedisperse/pallas_call | solution.py:182
  (59 shorter events, 21.7 us)
Async XLA Ops:
  0.0 10.7 %collective-permute-start = (bf16[2,64,128]{2,1,0:T(8,128)(2,1)}, bf16[2,64,128]{2,1,0:T(8,128)(2,1)S(1)}, u32[]{:S(2)}, u32[]{:S(2)}) collective-permute-start(bf16[2,64,128]{2,1,0:T(8,128)(2,1)} %param.8), channel_id=1, source_target_pairs={{0,4},{1,5},{2,6},{3,7},{4,0},{5,1},{6,2},{7,3},{8,12},{9,13},{10,... | collective-permute-start | bytes 98312 | tf_op jit(solution)/shard_map/ppermute | solution.py:223
  10.7 4.9 %copy-start.1 = (bf16[64,16,2048]{2,1,0:T(8,128)(2,1)}, bf16[64,16,2048]{2,1,0:T(8,128)(2,1)S(1)}, u32[]{:S(2)}) copy-start(bf16[64,16,2048]{2,1,0:T(8,128)(2,1)S(1)} %constant_dynamic-slice_fusion) | copy-start | bytes 12582916
  18.2 28.5 %all-to-all-start.2 = ((bf16[4,256,1024]{1,2,0:T(8,128)(2,1)}), bf16[4,256,1024]{1,2,0:T(8,128)(2,1)S(1)}, u32[]{:S(2)}, u32[]{:S(2)}) async-start(bf16[4,256,1024]{1,2,0:T(8,128)(2,1)} %copy.24), calls=%async_computation.2 | async-start | bytes 4194304 | tf_op jit(solution)/shard_map/all_to_all | solution.py:251
  24.3 2.2 %copy-start.2 = (bf16[64,16,2048]{2,1,0:T(8,128)(2,1)S(1)}, bf16[64,16,2048]{2,1,0:T(8,128)(2,1)}, u32[]{:S(2)}) copy-start(bf16[64,16,2048]{2,1,0:T(8,128)(2,1)} %copy-done.1) | copy-start | bytes 12582916
  32.3 18.8 %copy-start.4 = (s32[128,512]{1,0:T(8,128)S(1)}, s32[128,512]{1,0:T(8,128)}, u32[]{:S(2)}) copy-start(s32[128,512]{1,0:T(8,128)} %param.7) | copy-start | bytes 786436
  32.4 18.9 %copy-start.6 = (s32[512]{0:T(512)S(1)}, s32[512]{0:T(512)}, u32[]{:S(2)}) copy-start(s32[512]{0:T(512)} %param.6) | copy-start | bytes 6148
  32.4 20.4 %copy-start.5 = (bf16[2,64,128]{2,1,0:T(8,128)(2,1)S(1)}, bf16[2,64,128]{2,1,0:T(8,128)(2,1)}, u32[]{:S(2)}) copy-start(bf16[2,64,128]{2,1,0:T(8,128)(2,1)} %param.8) | copy-start | bytes 98308
  46.6 44.2 %all-to-all-start = ((bf16[4,256,1024]{1,2,0:T(8,128)(2,1)}), bf16[4,256,1024]{1,2,0:T(8,128)(2,1)}, u32[]{:S(2)}, u32[]{:S(2)}) async-start(bf16[4,256,1024]{1,2,0:T(8,128)(2,1)} %copy.13), calls=%async_computation | async-start | bytes 4194304 | tf_op jit(solution)/shard_map/all_to_all | solution.py:251
  90.8 44.3 %all-to-all-start.3 = ((bf16[32,4,32,128]{3,2,1,0:T(8,128)(2,1)}), bf16[32,4,32,128]{3,2,1,0:T(8,128)(2,1)S(1)}, u32[]{:S(2)}, u32[]{:S(2)}) async-start(bf16[32,4,32,128]{3,2,1,0:T(8,128)(2,1)} %bitcast.24), calls=%async_computation.3 | async-start | bytes 2097152 | tf_op jit(solution)/shard_map/all_to_all | solution.py:269
  131.9 9.9 %copy-start.7 = (s32[128]{0:T(128)S(1)}, s32[128]{0:T(128)}, u32[]{:S(2)}) copy-start(s32[128]{0:T(128)} %param.9) | copy-start | bytes 1540
  135.1 13.0 %copy-start = (bf16[32,4,32,128]{3,2,1,0:T(8,128)(2,1)}, bf16[32,4,32,128]{3,2,1,0:T(8,128)(2,1)S(1)}, u32[]{:S(2)}) copy-start(bf16[32,4,32,128]{3,2,1,0:T(8,128)(2,1)S(1)} %all-to-all-done.3) | copy-start | bytes 3145732
  135.1 33.1 %all-to-all-start.1 = ((bf16[32,4,32,128]{3,2,1,0:T(8,128)(2,1)}), bf16[32,4,32,128]{3,2,1,0:T(8,128)(2,1)S(1)}, u32[]{:S(2)}, u32[]{:S(2)}) async-start(bf16[32,4,32,128]{3,2,1,0:T(8,128)(2,1)} %bitcast.8), calls=%async_computation.1 | async-start | bytes 2097152 | tf_op jit(solution)/shard_map/all_to_all | solution.py:269
  168.2 1.0 copy-start.3

commit v2 on v1

--- a/solution.py
+++ b/solution.py
@@ -12,7 +12,7 @@
 NTAB = 64
 NDM = 32
 LANES = 128
-TILE = 64
+TILE = 16
 
 
 def phasor_rows(steps, channels):
@@ -84,19 +84,18 @@
     count = table_ref.shape[0]
     for tile in range(stations // TILE):
         span = pl.ds(tile * TILE, TILE)
-        real_at = index_ref[span, :]
-        imag_at = real_at + NTAB
-        for chan in range(count):
-            entry = jnp.broadcast_to(table_ref[pl.ds(chan, 1), :], (TILE, LANES))
-            for part, where in enumerate((real_at, imag_at)):
-                picked = pick_lanes(entry, where)
-                out_ref[chan, span, pl.ds(part * beams, beams)] = picked.astype(jnp.bfloat16)
+        for part in range(2):
+            where = (index_ref[span, :] + part * NTAB).astype(jnp.int16)
+            for chan in range(count):
+                entry = table_ref[pl.ds(chan, 1), :].astype(jnp.bfloat16)
+                picked = pick_lanes(jnp.broadcast_to(entry, (TILE, LANES)), where)
+                out_ref[chan, span, pl.ds(part * beams, beams)] = picked
 
 
 def station_weights(table, index):
     stations, beams = index.shape
     chans = table.shape[0]
-    block = min(8, chans)
+    block = min(16, chans)
     return pl.pallas_call(
         weight_kernel,
         grid=(chans // block,),
@@ -113,13 +112,28 @@
     )(table, index)
 
 
-def beam_kernel(signal_ref, weight_ref, out_ref):
-    count, depth, _ = signal_ref.shape
-    beams = out_ref.shape[2]
+def beam_kernel(signal_ref, weight_ref, out_ref, rows_ref):
+    peers, _, count, _ = signal_ref.shape
+    groups = rows_ref.shape[0]
+    shared = peers // groups
+    stations = LANES // shared
+    _, depth, beams = out_ref.shape
     half = depth // 2
+    for group in range(groups):
+        for part in range(2):
+            for frame in range(half):
+                pieces = [
+                    signal_ref[group * shared + peer, part, :, pl.ds(frame * stations, stations)]
+                    for peer in range(shared)
+                ]
+                piece = jnp.concatenate([p.astype(jnp.float32) for p in pieces], axis=1)
+                at = pl.ds(part * half + frame, count, stride=depth)
+                rows_ref[group, at, :] = piece
     for chan in range(count):
+        span = pl.ds(chan * depth, depth)
+        rows = jnp.concatenate([rows_ref[group, span, :] for group in range(groups)], axis=1)
         product = jnp.dot(
-            signal_ref[chan], weight_ref[chan], preferred_element_type=jnp.float32
+            rows.astype(jnp.bfloat16), weight_ref[chan], preferred_element_type=jnp.float32
         )
         real = product[:half, :beams] - product[half:, beams:]
         imag = product[half:, :beams] + product[:half, beams:]
@@ -128,18 +142,21 @@
 
 
 def form_beams(signal, weights):
-    chans, depth, held = signal.shape
-    beams = weights.shape[2] // 2
+    peers, _, chans, width = signal.shape
+    _, held, beams = weights.shape
+    beams = beams // 2
+    depth = 2 * width * peers // held
     block = min(16, chans)
     return pl.pallas_call(
         beam_kernel,
         grid=(chans // block,),
         in_specs=[
-            pl.BlockSpec((block, depth, held), lambda i: (i, 0, 0)),
+            pl.BlockSpec((peers, 2, block, width), lambda i: (0, 0, i, 0)),
             pl.BlockSpec((block, held, 2 * beams), lambda i: (i, 0, 0)),
         ],
         out_specs=pl.BlockSpec((block, depth, beams), lambda i: (i, 0, 0)),
         out_shape=jax.ShapeDtypeStruct((chans, depth, beams), jnp.bfloat16),
+        scratch_shapes=[pltpu.VMEM((held // LANES, block * depth, LANES), jnp.float32)],
         cost_estimate=pl.CostEstimate(
             flops=chans * depth * held * beams * 4,
             bytes_accessed=chans * held * beams * 6,
@@ -150,57 +167,57 @@
 
 
 def dedisperse_kernel(x_ref, cos_ref, sin_ref, fh_ref, fl_ref, ih_ref, il_ref, *rest):
-    out_ref = rest[-1]
-    sections, groups, blocks, _, depth, chans = x_ref.shape
+    *earlier, out_ref = rest
+    sections, groups, blocks, beams, depth, chans = x_ref.shape
     frames = cos_ref.shape[1]
+    done = 0
+    for ref in earlier:
+        out_ref[:, :, pl.ds(done, ref.shape[2])] = ref[...]
+        done += ref.shape[2]
 
     def dot(a, b):
         return jnp.dot(a, b, preferred_element_type=jnp.float32)
 
-    for block in range(blocks):
-        span = pl.ds(block * chans, chans)
-        x = x_ref[:, :, block, 0].reshape(sections * groups * depth, chans)
+    for beam in range(beams):
+        x = jnp.concatenate(
+            [
+                x_ref[:, :, block, beam].reshape(sections * groups * depth, chans)
+                for block in range(blocks)
+            ],
+            axis=1,
+        )
         spec = dot(fh_ref[...], x) + dot(fl_ref[...], x)
-        cosine = cos_ref[0, :, span]
-        sine = sin_ref[0, :, span]
+        cosine = cos_ref[beam]
+        sine = sin_ref[beam]
         real = spec[:frames] * cosine - spec[frames:] * sine
         imag = spec[:frames] * sine + spec[frames:] * cosine
         turned = jnp.concatenate((real, imag), axis=0)
         high = turned.astype(jnp.bfloat16)
         low = (turned - high.astype(jnp.float32)).astype(jnp.bfloat16)
         y = dot(ih_ref[...], high) + dot(ih_ref[...], low) + dot(il_ref[...], high)
-        out_ref[0, :, span] = y[:frames] * y[:frames] + y[frames:] * y[frames:]
-
-
-def dedisperse(series, cosine, sine, matrices, chunk, chunks, partial):
-    sections, groups, blocks, beams, depth, chans = series.shape
+        power = y[:frames] * y[:frames] + y[frames:] * y[frames:]
+        out_ref[beam, :, pl.ds(done, blocks * chans)] = power
+
+
+def dedisperse(series, cosine, sine, matrices, earlier):
+    _, _, blocks, beams, _, chans = series.shape
     frames = cosine.shape[1]
     wide = blocks * chans
-    whole = [pl.BlockSpec(m.shape, lambda i: (0, 0)) for m in matrices]
-    tables = pl.BlockSpec((1, frames, wide), lambda i: (i, 0, 0))
-    earlier = [] if partial is None else [partial]
+    operands = (series, cosine, sine, *matrices, *earlier)
+    total = wide + sum(part.shape[2] for part in earlier)
     return pl.pallas_call(
         dedisperse_kernel,
-        grid=(beams,),
-        in_specs=[
-            pl.BlockSpec(
-                (sections, groups, blocks, 1, depth, chans), lambda i: (0, 0, 0, i, 0, 0)
-            ),
-            tables,
-            tables,
-        ]
-        + whole
-        + [pl.BlockSpec(memory_space=pl.ANY) for _ in earlier],
-        out_specs=pl.BlockSpec((1, frames, wide), lambda i: (i, 0, chunk)),
-        out_shape=jax.ShapeDtypeStruct((beams, frames, wide * chunks), jnp.float32),
-        input_output_aliases={7: 0} if earlier else {},
+        in_specs=[pl.BlockSpec(memory_space=pltpu.VMEM) for _ in operands],
+        out_specs=pl.BlockSpec(memory_space=pltpu.VMEM),
+        out_shape=jax.ShapeDtypeStruct((beams, frames, total), jnp.float32),
         cost_estimate=pl.CostEstimate(
             flops=beams * wide * 2 * frames * 2 * frames * 14,
             bytes_accessed=beams * wide * frames * 16,
             transcendentals=0,
         ),
+        compiler_params=pltpu.CompilerParams(vmem_limit_bytes=24 << 20),
         name="dedisperse",
-    )(series, cosine, sine, *matrices, *earlier)
+    )(*operands)
 
 
 def body(voltages, station_map, beam_table, weight_table, dm_trial):
@@ -222,12 +239,11 @@
 
     swapped = lax.ppermute(weight_table, "dom", [(d, (d + peers) % doms) for d in range(doms)])
     block = lax.dynamic_slice_in_dim(voltages, section_index * local, local, 1)
-    rows = block.reshape(rows_here, NFFT)
+    rows = block.transpose(1, 0, 2).reshape(rows_here, NFFT)
 
     held = stations * peers
     mine = lax.dynamic_slice_in_dim(station_map, group_index * held, held, 0)
     arrival = jnp.take(beam_table, mine, axis=1, mode="clip").T
-    swapped, rows = lax.optimization_barrier((swapped, rows))
 
     column = jnp.arange(peers * 2 * chans, dtype=jnp.int32)
     column_chan = column // (2 * chans) * chans + column % chans
@@ -247,6 +263,8 @@
             table, rows, (((0,), (1,)), ((), ())), preferred_element_type=jnp.float32
         )
         spectrum = spectrum.astype(jnp.bfloat16).reshape(peers, 2 * chans, rows_here)
+        if chunk == 1:
+            swapped, spectrum = lax.optimization_barrier((swapped, spectrum))
         sent.append(
             lax.all_to_all(
                 spectrum,
@@ -257,13 +275,12 @@
                 tiled=True,
             )
         )
-    power = None
+    power = []
     for chunk in range(groups):
         owned_table = jnp.where(group_index == chunk, weight_table, swapped)
         lookup = owned_table.transpose(2, 0, 1).reshape(chans, 2 * NTAB).astype(jnp.float32)
         weights = station_weights(lookup, arrival)
-        signal = sent[chunk].reshape(peers, 2, chans, stations, local)
-        signal = signal.transpose(2, 1, 4, 0, 3).reshape(chans, 2 * local, held)
+        signal = sent[chunk].reshape(peers, 2, chans, rows_here)
         series = form_beams(signal, weights).transpose(2, 1, 0)
         series = series.reshape(sections * doms, per_device, 2 * local, chans)
         owned = lax.all_to_all(
@@ -275,10 +292,10 @@
         spread = 1.0 / (freq * freq * freq)
         coeff = math.pi * measure[:, None] * spread[None, :]
         phase = coeff[:, None, :] * (kappa * kappa / frames)[None, :, None]
-        power = dedisperse(
-            owned, jnp.cos(phase), jnp.sin(phase), matrices, chunk, groups, power
-        )
-    return power
+        cosine = jnp.cos(phase)
+        sine = jnp.sin(phase)
+        power = [dedisperse(owned, cosine, sine, matrices, power)]
+    return power[0]
 
 
 def solution(mesh):

time: 176 us -> 147 us (0.84)
  local copies, waits for them, and re-layouts: 38.6 us -> 16.6 us
  Pallas kernels: 64.5 us -> 47.2 us
  waiting for transfers between devices: 24.8 us -> 36.6 us
  other arithmetic: 13.7 us -> 10.5 us
    reshape x6 -> x0, local copies, waits for them, and re-layouts: 18.8 us -> none  [the longest x2 7.62 us: body(): signal = signal.transpose(2, 1, 4, 0, 3).reshape(chans, 2 * local, held)]
    ppermute x1, waiting for transfers between devices: 0.01 us -> 12.4 us  [body(): lax.ppermute(weight_table, 'dom', [(d, (d + peers) % doms) for d in range...]
    pallas_call x2, Pallas kernels: 32.1 us -> 19.7 us  [station_weights(): pl.pallas_call(weight_kernel, grid=(chans // block,), in_specs=[pl.BlockS...]
    all_to_all x2, waiting for transfers between devices: 10.3 us -> 2.24 us  [body(): lax.all_to_all(spectrum, 'dom', split_axis=0, concat_axis=0, axis_index_g...]
    all_to_all x2, waiting for transfers between devices: 14.5 us -> 21.9 us  [body(): lax.all_to_all(series, ('section', 'dom'), split_axis=0, concat_axis=0, t...]
    pallas_call x2, Pallas kernels: 11.1 us -> 4.03 us  [dedisperse(): pl.pallas_call(dedisperse_kernel, in_specs=[pl.BlockSpec(memory_space=plt...]
    transpose x2 -> x0, local copies, waits for them, and re-layouts: 4.52 us -> none  [body(): signal = signal.transpose(2, 1, 4, 0, 3).reshape(chans, 2 * local, held)]
    add x2 -> x0, other arithmetic: 2.49 us -> none  [dft_columns(): values = first[:, None, :] * cos_b[None] + second[:, None, :] * sin_b[None]]
  transfers between devices with their start and end apart: 5 -> 5, of which waited for: 2 -> 4; matrix products, arithmetic and copies ran while one was open for 30% -> 15% of each run, Pallas kernels for 34% -> 31%
where the time goes in v2:
time: 147 us; the launch traced here: 145 us
  Pallas kernels  47.2 us (32%)
  waiting for transfers between devices  36.6 us (25%)
  starting transfers between devices  22.6 us (15%)
  local copies, waits for them, and re-layouts  16.6 us (11%)
  matrix products  11.6 us (8%)
  other arithmetic  10.5 us (7%)
    pallas_call x2, Pallas kernels, form_beams(): pl.pallas_call(beam_kernel, grid=(chans // block,), in_specs=[pl.BlockSpe...  23.5 us
    all_to_all x2, waiting for transfers between devices, body(): lax.all_to_all(series, ('section', 'dom'), split_axis=0, concat_axis=0, t...  21.9 us
    pallas_call x2, Pallas kernels, station_weights(): pl.pallas_call(weight_kernel, grid=(chans // block,), in_specs=[pl.BlockS...  19.7 us
    ppermute x1, waiting for transfers between devices, body(): lax.ppermute(weight_table, 'dom', [(d, (d + peers) % doms) for d in range...  12.4 us
    dot_general x2, matrix products, body(): lax.dot_general(table, rows, (((0,), (1,)), ((), ())), preferred_element_...  11.6 us
    all_to_all x2, starting transfers between devices, body(): lax.all_to_all(spectrum, 'dom', split_axis=0, concat_axis=0, axis_index_g...  10.3 us
    all_to_all x2, starting transfers between devices, body(): lax.all_to_all(series, ('section', 'dom'), split_axis=0, concat_axis=0, t...  9.62 us
    transpose x2, local copies, waits for them, and re-layouts, body(): series = form_beams(signal, weights).transpose(2, 1, 0)  6.4 us
  transfers between devices with their start and end apart: 5, of which 4 were waited for; matrix products, arithmetic and copies ran while one was open for 15% of the time, Pallas kernels for 31%

profile of v2, /device:TPU:0, one launch (start us, length us, event | category | flops | bytes accessed | tf_op | source)
XLA Modules:
  0.0 145.3 jit_solution(14917379353217227139)
XLA Ops:
  2.3 2.5 %constant_dynamic-slice_fusion = bf16[64,16,2048]{2,1,0:T(8,128)(2,1)S(1)} fusion(bf16[64,64,2048]{2,1,0:T(8,128)(2,1)} %param.5, s32[]{:T(128)S(6)} %select_n.202), kind=kLoop, calls=%fused_computation.121 | loop fusion | bytes 8388612 | tf_op jit(solution)/shard_map/dynamic_slice | solution.py:241
  4.8 2.3 %copy.23 = bf16[64,16,2048]{2,0,1:T(8,128)(2,1)S(1)} copy(bf16[64,16,2048]{2,1,0:T(8,128)(2,1)S(1)} %constant_dynamic-slice_fusion) | data formatting | bytes 8388608
  8.4 5.9 %convolution_convert_fusion = bf16[1024,1024]{1,0:T(8,128)(2,1)} fusion(bf16[2048,1024]{1,0:T(8,128)(2,1)S(1)} %bitcast.43, bf16[1024,2048]{1,0:T(8,128)(2,1)S(1)} %bitcast.44), kind=kOutput, calls=%fused_computation.3 | convolution fusion | flops 4296015872 | bytes 10485760 | tf_op jit(solution)/shard_map/dot_general | solution.py:262
  14.3 5.4 %all-to-all-start.2 = ((bf16[4,256,1024]{2,1,0:T(8,128)(2,1)}), bf16[4,256,1024]{2,1,0:T(8,128)(2,1)S(1)}, u32[]{:S(2)}, u32[]{:S(2)}) async-start(bf16[4,256,1024]{2,1,0:T(8,128)(2,1)} %bitcast.47), calls=%async_computation.2 | async-start | bytes 4194304 | tf_op jit(solution)/shard_map/all_to_all | solution.py:269
  19.7 2.7 %collective-permute-start = (bf16[2,64,128]{2,1,0:T(8,128)(2,1)S(1)}, bf16[2,64,128]{2,1,0:T(8,128)(2,1)S(1)}, u32[]{:S(2)}, u32[]{:S(2)}) collective-permute-start(bf16[2,64,128]{2,1,0:T(8,128)(2,1)S(1)} %copy-done.6), channel_id=1, source_target_pairs={{0,4},{1,5},{2,6},{3,7},{4,0},{5,1},{6,2},{7,3},{8,12},{9,13},{10,... | collective-permute-start | bytes 98312 | tf_op jit(solution)/shard_map/ppermute | solution.py:240
  23.4 1.5 %multiply_convert_fusion.1 = bf16[32,64,1024]{2,1,0:T(8,128)(2,1)S(1)} fusion(f32[32,64]{1,0:T(8,128)S(1)} %subtract_multiply_fusion, f32[64,1024]{1,0:T(8,128)S(1)} %get-tuple-element.20, f32[32,1024]{1,0:T(8,128)S(1)} %get-tuple-element.19, f32[64,1024]{1,0:T(8,128)S(1)} %get-tuple-element.18, f32[32,1024]{1,0:T(8,128)S(1)} %get-tuple-element.17), kind=kLoop, calls=%fused_computation.2 | loop fusion | flops 10485760 | bytes 4988928 | tf_op jit(solution)/shard_map/convert_element_type | solution.py:39
  24.9 5.7 %convolution_convert_fusion.1 = bf16[1024,1024]{1,0:T(8,128)(2,1)} fusion(bf16[2048,1024]{1,0:T(8,128)(2,1)S(1)} %bitcast.42, bf16[1024,2048]{1,0:T(8,128)(2,1)S(1)} %bitcast.45), kind=kOutput, calls=%fused_computation.4 | convolution fusion | flops 4296015872 | bytes 10485760 | tf_op jit(solution)/shard_map/dot_general | solution.py:262
  30.7 12.4 %collective-permute-done = bf16[2,64,128]{2,1,0:T(8,128)(2,1)S(1)} collective-permute-done((bf16[2,64,128]{2,1,0:T(8,128)(2,1)S(1)}, bf16[2,64,128]{2,1,0:T(8,128)(2,1)S(1)}, u32[]{:S(2)}, u32[]{:S(2)}) %collective-permute-start) | collective-permute-done | bytes 32800 | tf_op jit(solution)/shard_map/ppermute | solution.py:240
  43.1 2.2 %all-to-all-done.2 = bf16[4,256,1024]{2,1,0:T(8,128)(2,1)S(1)} async-done(((bf16[4,256,1024]{2,1,0:T(8,128)(2,1)}), bf16[4,256,1024]{2,1,0:T(8,128)(2,1)S(1)}, u32[]{:S(2)}, u32[]{:S(2)}) %all-to-all-start.2) | async-done | bytes 2097184 | tf_op jit(solution)/shard_map/all_to_all | solution.py:269
  45.3 4.9 %all-to-all-start = ((bf16[4,256,1024]{2,1,0:T(8,128)(2,1)}), bf16[4,256,1024]{2,1,0:T(8,128)(2,1)}, u32[]{:S(2)}, u32[]{:S(2)}) async-start(bf16[4,256,1024]{2,1,0:T(8,128)(2,1)} %bitcast.46), calls=%async_computation | async-start | bytes 4194304 | tf_op jit(solution)/shard_map/all_to_all | solution.py:269
  50.4 1.3 gather_fusion
  52.5 9.9 %station_weights.3.weight_ref = bf16[128,256,256]{2,1,0:T(8,128)(2,1)} custom-call(f32[128,128]{1,0:T(8,128)} %copy.21.table_ref, s32[256,128]{1,0:T(8,128)} %gather_fusion), custom_call_target="tpu_custom_call" | custom-call | bytes 41943040 | tf_op jit(solution)/shard_map/station_weights/pallas_call | solution.py:99
  62.4 11.7 %form_beams.3 = bf16[128,32,128]{2,1,0:T(8,128)(2,1)} custom-call(bf16[4,2,128,1024]{3,2,1,0:T(8,128)(2,1)} %bitcast.39, bf16[128,256,256]{2,1,0:T(8,128)(2,1)} %station_weights.3.weight_ref), custom_call_target="tpu_custom_call" | custom-call | flops 536870912 | bytes 25165824 | tf_op jit(solution)/shard_map/form_beams/pallas_call | solution.py:150
  74.1 3.2 %copy.22 = bf16[128,32,128]{2,1,0:T(8,128)(2,1)} copy(bf16[128,32,128]{0,1,2:T(8,128)(2,1)} %bitcast.40) | data formatting | bytes 2097152 | tf_op jit(solution)/shard_map/transpose | solution.py:284
  77.3 5.5 %all-to-all-start.3 = ((bf16[32,4,32,128]{3,2,1,0:T(8,128)(2,1)}), bf16[32,4,32,128]{3,2,1,0:T(8,128)(2,1)S(1)}, u32[]{:S(2)}, u32[]{:S(2)}) async-start(bf16[32,4,32,128]{3,2,1,0:T(8,128)(2,1)} %bitcast.24), calls=%async_computation.3 | async-start | bytes 2097152 | tf_op jit(solution)/shard_map/all_to_all | solution.py:286
  83.6 9.9 %station_weights.2.weight_ref = bf16[128,256,256]{2,1,0:T(8,128)(2,1)} custom-call(f32[128,128]{1,0:T(8,128)} %copy.14.table_ref, s32[256,128]{1,0:T(8,128)} %gather_fusion), custom_call_target="tpu_custom_call" | custom-call | bytes 41943040 | tf_op jit(solution)/shard_map/station_weights/pallas_call | solution.py:99
  93.5 11.7 %form_beams.2 = bf16[128,32,128]{2,1,0:T(8,128)(2,1)} custom-call(bf16[4,2,128,1024]{3,2,1,0:T(8,128)(2,1)} %bitcast.4.signal_ref, bf16[128,256,256]{2,1,0:T(8,128)(2,1)} %station_weights.2.weight_ref), custom_call_target="tpu_custom_call" | custom-call | flops 536870912 | bytes 25165824 | tf_op jit(solution)/shard_map/form_beams/pallas_call | solution.py:150
  105.2 3.2 %copy.15 = bf16[128,32,128]{2,1,0:T(8,128)(2,1)} copy(bf16[128,32,128]{0,1,2:T(8,128)(2,1)} %bitcast.41) | data formatting | bytes 2097152 | tf_op jit(solution)/shard_map/transpose | solution.py:284
  108.4 1.9 %all-to-all-done.3 = bf16[32,4,32,128]{3,2,1,0:T(8,128)(2,1)S(1)} async-done(((bf16[32,4,32,128]{3,2,1,0:T(8,128)(2,1)}), bf16[32,4,32,128]{3,2,1,0:T(8,128)(2,1)S(1)}, u32[]{:S(2)}, u32[]{:S(2)}) %all-to-all-start.3) | async-done | bytes 1048608 | tf_op jit(solution)/shard_map/all_to_all | solution.py:286
  110.3 4.1 %all-to-all-start.1 = ((bf16[32,4,32,128]{3,2,1,0:T(8,128)(2,1)}), bf16[32,4,32,128]{3,2,1,0:T(8,128)(2,1)S(1)}, u32[]{:S(2)}, u32[]{:S(2)}) async-start(bf16[32,4,32,128]{3,2,1,0:T(8,128)(2,1)} %bitcast.8), calls=%async_computation.1 | async-start | bytes 2097152 | tf_op jit(solution)/shard_map/all_to_all | solution.py:286
  115.7 3.7 %multiply_sine_fusion = (f32[4,64,512]{2,1,0:T(8,128)S(1)}, f32[4,64,512]{2,1,0:T(8,128)S(1)}, f32[4,64,512]{2,1,0:T(8,128)S(1)}, f32[4,64,512]{2,1,0:T(8,128)S(1)}) fusion(f32[4,512]{1,0:T(4,128)S(1)} %get-tuple-element.57, f32[64]{0:T(128)S(1)} %fusion.56, f32[4,512]{1,0:T(4,128)S(1)} %get-tuple-element.58), kind=kLoop, calls=%fused_computation.5 | loop fusion | flops 262144 | bytes 2113792 | tf_op jit(solution)/shard_map/sin | solution.py:296
  119.4 1.5 %dedisperse.2.rest_0_ = f32[4,64,512]{2,1,0:T(8,128)S(1)} custom-call(bf16[4,2,4,4,32,128]{5,4,3,2,1,0:T(8,128)(2,1)S(1)} %bitcast.37, f32[4,64,512]{2,1,0:T(8,128)S(1)} %get-tuple-element.42.cos_ref, f32[4,64,512]{2,1,0:T(8,128)S(1)} %get-tuple-element.41.sin_ref, bf16[128,256]{1,0:T(8,128)(2,1)S(1)} %get-tuple-element.30.fh_ref, ...), custom_call_target="tpu_custom_call" | custom-call | flops 469762048 | bytes 2097152 | tf_op jit(solution)/shard_map/dedisperse/pallas_call | solution.py:208
  121.7 20.0 %all-to-all-done.1 = bf16[32,4,32,128]{3,2,1,0:T(8,128)(2,1)S(1)} async-done(((bf16[32,4,32,128]{3,2,1,0:T(8,128)(2,1)}), bf16[32,4,32,128]{3,2,1,0:T(8,128)(2,1)S(1)}, u32[]{:S(2)}, u32[]{:S(2)}) %all-to-all-start.1) | async-done | bytes 1048608 | tf_op jit(solution)/shard_map/all_to_all | solution.py:286
  142.8 2.5 %dedisperse.3 = f32[4,64,1024]{2,1,0:T(8,128)} custom-call(bf16[4,2,4,4,32,128]{5,4,3,2,1,0:T(8,128)(2,1)S(1)} %bitcast.38, f32[4,64,512]{2,1,0:T(8,128)S(1)} %get-tuple-element.55.cos_ref, f32[4,64,512]{2,1,0:T(8,128)S(1)} %get-tuple-element.56.sin_ref, bf16[128,256]{1,0:T(8,128)(2,1)S(1)} %get-tuple-element.30.fh_ref, ...), custom_call_target="tpu_custom_call" | custom-call | flops 469762048 | bytes 2097152 | tf_op jit(solution)/shard_map/dedisperse/pallas_call | solution.py:208
  (50 shorter events, 9.3 us)
Async XLA Ops:
  7.1 7.2 %copy-start.3 = (bf16[64,16,2048]{2,0,1:T(8,128)(2,1)}, bf16[64,16,2048]{2,0,1:T(8,128)(2,1)S(1)}, u32[]{:S(2)}) copy-start(bf16[64,16,2048]{2,0,1:T(8,128)(2,1)S(1)} %copy.23) | copy-start | bytes 12582916
  14.3 5.4 %copy-start.6 = (bf16[2,64,128]{2,1,0:T(8,128)(2,1)S(1)}, bf16[2,64,128]{2,1,0:T(8,128)(2,1)}, u32[]{:S(2)}) copy-start(bf16[2,64,128]{2,1,0:T(8,128)(2,1)} %param.8) | copy-start | bytes 98308
  14.3 31.0 %all-to-all-start.2 = ((bf16[4,256,1024]{2,1,0:T(8,128)(2,1)}), bf16[4,256,1024]{2,1,0:T(8,128)(2,1)S(1)}, u32[]{:S(2)}, u32[]{:S(2)}) async-start(bf16[4,256,1024]{2,1,0:T(8,128)(2,1)} %bitcast.47), calls=%async_computation.2 | async-start | bytes 4194304 | tf_op jit(solution)/shard_map/all_to_all | solution.py:269
  19.7 5.2 %copy-start.4 = (bf16[64,16,2048]{2,0,1:T(8,128)(2,1)S(1)}, bf16[64,16,2048]{2,0,1:T(8,128)(2,1)}, u32[]{:S(2)}) copy-start(bf16[64,16,2048]{2,0,1:T(8,128)(2,1)} %copy-done.3) | copy-start | bytes 12582916
  19.7 23.4 %collective-permute-start = (bf16[2,64,128]{2,1,0:T(8,128)(2,1)S(1)}, bf16[2,64,128]{2,1,0:T(8,128)(2,1)S(1)}, u32[]{:S(2)}, u32[]{:S(2)}) collective-permute-start(bf16[2,64,128]{2,1,0:T(8,128)(2,1)S(1)} %copy-done.6), channel_id=1, source_target_pairs={{0,4},{1,5},{2,6},{3,7},{4,0},{5,1},{6,2},{7,3},{8,12},{9,13},{10,... | collective-permute-start | bytes 98312 | tf_op jit(solution)/shard_map/ppermute | solution.py:240
  30.7 19.5 %copy-start.5 = (s32[128,512]{1,0:T(8,128)S(1)}, s32[128,512]{1,0:T(8,128)}, u32[]{:S(2)}) copy-start(s32[128,512]{1,0:T(8,128)} %param.7) | copy-start | bytes 786436
  30.7 19.7 %copy-start.7 = (s32[512]{0:T(512)S(1)}, s32[512]{0:T(512)}, u32[]{:S(2)}) copy-start(s32[512]{0:T(512)} %param.6) | copy-start | bytes 6148
  45.3 17.1 %copy-start.2 = (bf16[4,256,1024]{2,1,0:T(8,128)(2,1)}, bf16[4,256,1024]{2,1,0:T(8,128)(2,1)S(1)}, u32[]{:S(2)}) copy-start(bf16[4,256,1024]{2,1,0:T(8,128)(2,1)S(1)} %all-to-all-done.2) | copy-start | bytes 6291460
  45.3 32.0 %all-to-all-start = ((bf16[4,256,1024]{2,1,0:T(8,128)(2,1)}), bf16[4,256,1024]{2,1,0:T(8,128)(2,1)}, u32[]{:S(2)}, u32[]{:S(2)}) async-start(bf16[4,256,1024]{2,1,0:T(8,128)(2,1)} %bitcast.46), calls=%async_computation | async-start | bytes 4194304 | tf_op jit(solution)/shard_map/all_to_all | solution.py:269
  77.3 33.0 %all-to-all-start.3 = ((bf16[32,4,32,128]{3,2,1,0:T(8,128)(2,1)}), bf16[32,4,32,128]{3,2,1,0:T(8,128)(2,1)S(1)}, u32[]{:S(2)}, u32[]{:S(2)}) async-start(bf16[32,4,32,128]{3,2,1,0:T(8,128)(2,1)} %bitcast.24), calls=%async_computation.3 | async-start | bytes 2097152 | tf_op jit(solution)/shard_map/all_to_all | solution.py:286
  105.2 10.3 %copy-start.8 = (s32[128]{0:T(128)S(1)}, s32[128]{0:T(128)}, u32[]{:S(2)}) copy-start(s32[128]{0:T(128)} %param.9) | copy-start | bytes 1540
  110.3 31.4 %all-to-all-start.1 = ((bf16[32,4,32,128]{3,2,1,0:T(8,128)(2,1)}), bf16[32,4,32,128]{3,2,1,0:T(8,128)(2,1)S(1)}, u32[]{:S(2)}, u32[]{:S(2)}) async-start(bf16[32,4,32,128]{3,2,1,0:T(8,128)(2,1)} %bitcast.8), calls=%async_computation.1 | async-start | bytes 2097152 | tf_op jit(solution)/shard_map/all_to_all | solution.py:286
  120.9 0.8 copy-start
  141.7 1.0 copy-start.1
